TPU v7x, 256 devices: a whole 4x4x8 slice. The times are simulated.
256 devices in a mesh: gx: 8 (over x, core), gy: 4 (over y), gz: 8 (over z).
Axes of the slice: x: 4, y: 4, z: 8, core: 2. Of those that a mesh axis runs over, the one named last changes fastest.
Arguments:
- facies: int32 [128, 128, 512], P('gz', 'gx', 'gy'), may hold values from 0 to 15
- perm_table: float32 [3, 16], replicated, may hold values from 0.0003 to 3, as said below
- line_breaks: int32 [127], replicated, may hold values 0 or 1
Outputs:
- pressure: float32 [3, 128, 128, 512], P(None, 'gz', 'gx', 'gy')
- residual: float32 [3, 128, 128, 512], P(None, 'gz', 'gx', 'gy')
Inputs may be any that keep to these rules, and one draw needn't show every extreme that they name: `perm_table`: positive coefficients.
All inputs are finite; a program needn't handle non-finite values.
Results may differ from a plain program's by a relative error of at most 0.0003.
Values sent between devices are 32-bit elements; how exact they have to be, the bound alone decides.
A program may use at most 64 MiB of HBM per device.

v0:
```python
import jax
import jax.numpy as jnp
from jax import lax
from jax.sharding import PartitionSpec as P


def with_halo(x, sides, width):
    for axis, dim in sides:
        size, length = (lax.axis_size(axis), x.shape[dim])
        up = [(i, (i + 1) % size) for i in range(size - 1)]
        down = [(j, i) for i, j in up]
        last = lax.slice_in_dim(x, length - width, length, axis=dim)
        leading = lax.slice_in_dim(x, 0, width, axis=dim)
        before = lax.ppermute(last, axis, up)
        after = lax.ppermute(leading, axis, down)
        x = jnp.concatenate([before, x, after], axis=dim)
    return x


def from_behind(block, axis, distance):
    devices = range(lax.axis_size(axis))
    route = [(i - distance, i) for i in devices if i - distance in devices]
    return lax.ppermute(block, axis, route)


def six_sides(padded):
    return (
        padded[..., :-2, 1:-1, 1:-1],
        padded[..., 2:, 1:-1, 1:-1],
        padded[..., 1:-1, :-2, 1:-1],
        padded[..., 1:-1, 2:, 1:-1],
        padded[..., 1:-1, 1:-1, :-2],
        padded[..., 1:-1, 1:-1, 2:],
    )


def face_pair(centre, beside):
    inside = beside > 0.0
    harmonic = 2.0 * centre * beside / (centre + beside)
    return (
        jnp.where(inside, harmonic, 2.0 * centre),
        jnp.where(inside, harmonic, centre),
        jnp.where(inside, harmonic, 0.0),
    )


def assemble(perm, padded):
    z_sides = six_sides(padded[2])
    x_sides = six_sides(padded[0])
    y_sides = six_sides(padded[1])
    z_low = face_pair(perm[2], z_sides[0])
    z_high = face_pair(perm[2], z_sides[1])
    x_low = face_pair(perm[0], x_sides[2])
    x_high = face_pair(perm[0], x_sides[3])
    y_low = face_pair(perm[1], y_sides[4])
    y_high = face_pair(perm[1], y_sides[5])
    taus = (z_low[0], z_high[0], x_low[0], x_high[0], y_low[0], y_high[0])
    source = jnp.stack([x_high[1] - x_low[1], y_high[1] - y_low[1], z_high[1] - z_low[1]])
    centre_sum = taus[0] + taus[1] + taus[2] + taus[3] + taus[4] + taus[5]
    return (taus, source, centre_sum, z_low[2], z_high[2])


def explicit_terms(taus, sides, break_low, break_high):
    return (
        taus[2] * sides[2]
        + taus[3] * sides[3]
        + taus[4] * sides[4]
        + taus[5] * sides[5]
        + taus[0] * break_low * sides[0]
        + taus[1] * break_high * sides[1]
    )


def residual_of(taus, sides, source, centre_sum, field):
    total = (
        taus[0] * sides[0]
        + taus[1] * sides[1]
        + taus[2] * sides[2]
        + taus[3] * sides[3]
        + taus[4] * sides[4]
        + taus[5] * sides[5]
    )
    return source - centre_sum * field + total


def table_lookup(facies, perm_table):
    perm = jnp.zeros((3,) + facies.shape, jnp.float32)
    for label in range(perm_table.shape[1]):
        perm = jnp.where((facies == label)[None], perm_table[:, label][:, None, None, None], perm)
    return perm


def widened(field):
    return with_halo(field, (("gx", 2), ("gy", 3), ("gz", 1)), 1)


def shift_rows(values, stride, fill, axis):
    count = values.shape[axis]
    step = abs(stride)
    filler = jnp.full_like(lax.slice_in_dim(values, 0, step, axis=axis), fill)
    if stride > 0:
        return jnp.concatenate([filler, lax.slice_in_dim(values, 0, count - step, axis=axis)], axis)
    return jnp.concatenate([lax.slice_in_dim(values, step, count, axis=axis), filler], axis)


def interior_solve(sub_diag, main_diag, super_diag, columns):
    stride = 1
    count = main_diag.shape[0]
    while stride < count:
        sub_low = shift_rows(sub_diag, stride, 0.0, 0)
        super_low = shift_rows(super_diag, stride, 0.0, 0)
        main_low = shift_rows(main_diag, stride, 1.0, 0)
        column_low = shift_rows(columns, stride, 0.0, 1)
        sub_high = shift_rows(sub_diag, -stride, 0.0, 0)
        super_high = shift_rows(super_diag, -stride, 0.0, 0)
        main_high = shift_rows(main_diag, -stride, 1.0, 0)
        column_high = shift_rows(columns, -stride, 0.0, 1)
        left = sub_diag / main_low
        right = super_diag / main_high
        main_diag = main_diag - left * super_low - right * sub_high
        columns = columns - left[None] * column_low - right[None] * column_high
        sub_diag = -left * sub_low
        super_diag = -right * super_high
        stride *= 2
    return columns / main_diag[None]


def block_product(left, right):
    return jnp.stack(
        [
            left[0] * right[0] + left[1] * right[2],
            left[0] * right[1] + left[1] * right[3],
            left[2] * right[0] + left[3] * right[2],
            left[2] * right[1] + left[3] * right[3],
        ]
    )


def block_inverse(block):
    determinant = block[0] * block[3] - block[1] * block[2]
    return jnp.stack([block[3], -block[1], -block[2], block[0]]) / determinant


def block_apply(block, pair):
    return jnp.stack(
        [
            block[0][None] * pair[0] + block[1][None] * pair[1],
            block[2][None] * pair[0] + block[3][None] * pair[1],
        ]
    )


def cyclic_reduce(blocks, pair):
    sub_block, mid_block, sup_block = blocks
    count = lax.axis_size("gz")
    position = lax.axis_index("gz")
    solid = jnp.ones_like(mid_block[0])
    empty = jnp.zeros_like(mid_block[0])
    unit = jnp.stack([solid, empty, empty, solid])
    stride = 1
    while stride < count:
        below = from_behind((sub_block, mid_block, sup_block, pair), "gz", stride)
        above = from_behind((sub_block, mid_block, sup_block, pair), "gz", -stride)
        mid_below = jnp.where(position >= stride, below[1], unit)
        mid_above = jnp.where(position + stride < count, above[1], unit)
        left_factor = -block_product(sub_block, block_inverse(mid_below))
        right_factor = -block_product(sup_block, block_inverse(mid_above))
        mid_block = (
            mid_block + block_product(left_factor, below[2]) + block_product(right_factor, above[0])
        )
        pair = pair + block_apply(left_factor, below[3]) + block_apply(right_factor, above[3])
        sub_block = block_product(left_factor, below[0])
        sup_block = block_product(right_factor, above[2])
        stride *= 2
    return block_apply(block_inverse(mid_block), pair)


def per_device(facies, perm_table, line_breaks):
    depth = facies.shape[0]
    inner = depth - 2
    perm = table_lookup(facies, perm_table)
    padded = with_halo(perm, (("gx", 2), ("gy", 3), ("gz", 1)), 1)
    taus, source, centre_sum, link_low, link_high = assemble(perm, padded)
    extended = jnp.concatenate(
        [jnp.zeros((1,), jnp.int32), line_breaks, jnp.zeros((1,), jnp.int32)]
    ).astype(jnp.float32)
    window = lax.dynamic_slice_in_dim(extended, lax.axis_index("gz") * depth, depth + 1)
    break_low = window[:depth][:, None, None]
    break_high = window[1:][:, None, None]
    sub_diag = -link_low * (1.0 - break_low)
    super_diag = -link_high * (1.0 - break_high)
    single_row = jnp.zeros_like(sub_diag[1:2])
    blank = jnp.zeros((inner - 1,) + sub_diag.shape[1:], jnp.float32)
    inner_sub = jnp.concatenate([single_row, sub_diag[2 : depth - 1]])
    inner_super = jnp.concatenate([super_diag[1 : depth - 2], single_row])
    inner_main = centre_sum[1 : depth - 1]
    push_low = jnp.concatenate([-sub_diag[1:2], blank])
    push_high = jnp.concatenate([blank, -super_diag[depth - 2 : depth - 1]])
    columns = jnp.concatenate([source[:, 1 : depth - 1], push_low[None], push_high[None]])
    solved = interior_solve(inner_sub, inner_main, inner_super, columns)
    inner_first = solved[:3]
    weight_low = solved[3]
    weight_high = solved[4]
    lower_u = sub_diag[0]
    centre_u = centre_sum[0] + super_diag[0] * weight_low[0]
    upper_u = super_diag[0] * weight_high[0]
    lower_v = sub_diag[depth - 1] * weight_low[inner - 1]
    centre_v = centre_sum[depth - 1] + sub_diag[depth - 1] * weight_high[inner - 1]
    upper_v = super_diag[depth - 1]

    def reduced_source(right, interior):
        return jnp.stack(
            [
                right[:, 0] - super_diag[0][None] * interior[:, 0],
                right[:, depth - 1] - sub_diag[depth - 1][None] * interior[:, inner - 1],
            ]
        )

    def rebuild(interior, ends):
        middle = (
            interior + weight_low[None] * ends[0][:, None] + weight_high[None] * ends[1][:, None]
        )
        return jnp.concatenate([ends[0][:, None], middle, ends[1][:, None]], axis=1)

    nothing = jnp.zeros_like(lower_u)
    blocks = (
        jnp.stack([nothing, lower_u, nothing, nothing]),
        jnp.stack([centre_u, upper_u, lower_v, centre_v]),
        jnp.stack([nothing, nothing, upper_v, nothing]),
    )

    def solve_reduced(pair):
        return cyclic_reduce(blocks, pair)

    first = rebuild(inner_first, solve_reduced(reduced_source(source, inner_first)))
    right = source + explicit_terms(taus, six_sides(widened(first)), break_low, break_high)
    inner_second = interior_solve(inner_sub, inner_main, inner_super, right[:, 1 : depth - 1])
    second = rebuild(inner_second, solve_reduced(reduced_source(right, inner_second)))
    residual = residual_of(taus, six_sides(widened(second)), source, centre_sum, second)
    return (second, residual)


def solution(mesh):
    return jax.shard_map(
        per_device,
        mesh=mesh,
        in_specs=(P("gz", "gx", "gy"), P(), P()),
        out_specs=(P(None, "gz", "gx", "gy"), P(None, "gz", "gx", "gy")),
        check_vma=False,
    )
```

profile of v0, /device:TPU:62, one launch (start us, length us, event | category | flops | bytes accessed | tf_op | source)
XLA Modules:
  0.0 237.5 jit_solution(3278803844513645728)
XLA Ops:
  17.4 3.8 %collective-permute-done.2 = f32[3,16,18,1]{2,1,3,0:T(8,128)S(1)} collective-permute-done((f32[3,16,18,1]{2,1,3,0:T(8,128)S(1)}, f32[3,16,18,1]{2,1,3,0:T(8,128)S(1)}, u32[]{:S(2)}, u32[]{:S(2)}) %collective-permute-start.2) | collective-permute-done | bytes 3488 | tf_op jit(solution)/shard_map/ppermute | solution.py:14
  22.2 3.8 %collective-permute-start.4 = (f32[3,1,18,130]{3,1,2,0:T(1,128)S(1)}, f32[3,1,18,130]{3,1,2,0:T(1,128)S(1)}, u32[]{:S(2)}, u32[]{:S(2)}) collective-permute-start(f32[3,1,18,130]{3,1,2,0:T(1,128)S(1)} %get-tuple-element.92), channel_id=1, source_target_pairs={{0,1},{1,2},{2,3},{3,4},{4,5},{5,6},{6,7},{8,9},{9,10},{10,11},{11... | collective-permute-start | bytes 84248 | tf_op jit(solution)/shard_map/ppermute | solution.py:14
  28.7 3.4 %collective-permute-done.5 = f32[3,1,18,130]{3,1,2,0:T(1,128)S(1)} collective-permute-done((f32[3,1,18,130]{3,1,2,0:T(1,128)S(1)}, f32[3,1,18,130]{3,1,2,0:T(1,128)S(1)}, u32[]{:S(2)}, u32[]{:S(2)}) %collective-permute-start.5) | collective-permute-done | bytes 28112 | tf_op jit(solution)/shard_map/ppermute | solution.py:15
  38.6 4.8 %collective-permute-start.6 = (f32[4,16,128]{2,1,0:T(8,128)S(1)}, f32[4,16,128]{2,1,0:T(8,128)S(1)}, u32[]{:S(2)}, u32[]{:S(2)}) collective-permute-start(f32[4,16,128]{2,1,0:T(8,128)S(1)} %pad_maximum_fusion.55), channel_id=1, source_target_pairs={{0,1},{1,2},{2,3},{3,4},{4,5},{5,6},{6,7},{8,9},{9,10},{10,11},{11... | collective-permute-start | bytes 98312 | tf_op jit(solution)/shard_map/ppermute | solution.py:23
  47.1 5.1 %collective-permute-start.10 = (f32[4,16,128]{2,1,0:T(8,128)S(1)}, f32[4,16,128]{2,1,0:T(8,128)S(1)}, u32[]{:S(2)}, u32[]{:S(2)}) collective-permute-start(f32[4,16,128]{2,1,0:T(8,128)S(1)} %get-tuple-element.335), channel_id=1, source_target_pairs={{0,1},{1,2},{2,3},{3,4},{4,5},{5,6},{6,7},{8,9},{9,10},{10,11},{11... | collective-permute-start | bytes 98312 | tf_op jit(solution)/shard_map/ppermute | solution.py:23
  52.2 5.1 %collective-permute-start.7 = (f32[4,16,128]{2,1,0:T(8,128)S(1)}, f32[4,16,128]{2,1,0:T(8,128)S(1)}, u32[]{:S(2)}, u32[]{:S(2)}) collective-permute-start(f32[4,16,128]{2,1,0:T(8,128)S(1)} %get-tuple-element.336), channel_id=1, source_target_pairs={{0,1},{1,2},{2,3},{3,4},{4,5},{5,6},{6,7},{8,9},{9,10},{10,11},{11... | collective-permute-start | bytes 98312 | tf_op jit(solution)/shard_map/ppermute | solution.py:23
  60.3 8.2 %collective-permute-start.11 = (f32[4,16,128]{2,1,0:T(8,128)S(1)}, f32[4,16,128]{2,1,0:T(8,128)S(1)}, u32[]{:S(2)}, u32[]{:S(2)}) collective-permute-start(f32[4,16,128]{2,1,0:T(8,128)S(1)} %fusion.64), channel_id=1, source_target_pairs={{0,2},{1,3},{2,4},{3,5},{4,6},{5,7},{8,10},{9,11},{10,12},{11,13},... | collective-permute-start | bytes 98312 | tf_op jit(solution)/shard_map/ppermute | solution.py:23
  68.5 4.8 %collective-permute-start.22 = (f32[2,3,16,128]{3,2,1,0:T(8,128)S(1)}, f32[2,3,16,128]{3,2,1,0:T(8,128)S(1)}, u32[]{:S(2)}, u32[]{:S(2)}) collective-permute-start(f32[2,3,16,128]{3,2,1,0:T(8,128)S(1)} %pad_maximum_fusion.53), channel_id=1, source_target_pairs={{0,1},{1,2},{2,3},{3,4},{4,5},{5,6},{6,7},{8,9},{9,10},{10,11},{11... | collective-permute-start | bytes 147464 | tf_op jit(solution)/shard_map/ppermute | solution.py:23
  77.3 3.8 %collective-permute-done.12 = f32[4,16,128]{2,1,0:T(8,128)S(1)} collective-permute-done((f32[4,16,128]{2,1,0:T(8,128)S(1)}, f32[4,16,128]{2,1,0:T(8,128)S(1)}, u32[]{:S(2)}, u32[]{:S(2)}) %collective-permute-start.12) | collective-permute-done | bytes 32800 | tf_op jit(solution)/shard_map/ppermute | solution.py:23
  82.5 7.0 %collective-permute-start.16 = (f32[4,16,128]{2,1,0:T(8,128)S(1)}, f32[4,16,128]{2,1,0:T(8,128)S(1)}, u32[]{:S(2)}, u32[]{:S(2)}) collective-permute-start(f32[4,16,128]{2,1,0:T(8,128)S(1)} %pad_maximum_fusion.59), channel_id=1, source_target_pairs={{0,2},{1,3},{2,4},{3,5},{4,6},{5,7},{8,10},{9,11},{10,12},{11,13},... | collective-permute-start | bytes 98312 | tf_op jit(solution)/shard_map/ppermute | solution.py:23
  89.6 6.0 %collective-permute-start.13 = (f32[4,16,128]{2,1,0:T(8,128)S(1)}, f32[4,16,128]{2,1,0:T(8,128)S(1)}, u32[]{:S(2)}, u32[]{:S(2)}) collective-permute-start(f32[4,16,128]{2,1,0:T(8,128)S(1)} %pad_maximum_fusion.58), channel_id=1, source_target_pairs={{0,2},{1,3},{2,4},{3,5},{4,6},{5,7},{8,10},{9,11},{10,12},{11,13},... | collective-permute-start | bytes 98312 | tf_op jit(solution)/shard_map/ppermute | solution.py:23
  98.6 8.5 %collective-permute-start.17 = (f32[4,16,128]{2,1,0:T(8,128)S(1)}, f32[4,16,128]{2,1,0:T(8,128)S(1)}, u32[]{:S(2)}, u32[]{:S(2)}) collective-permute-start(f32[4,16,128]{2,1,0:T(8,128)S(1)} %fusion.65), channel_id=1, source_target_pairs={{0,4},{1,5},{2,6},{3,7},{8,12},{9,13},{10,14},{11,15},{16,20},{17,... | collective-permute-start | bytes 98312 | tf_op jit(solution)/shard_map/ppermute | solution.py:23
  107.0 5.1 %collective-permute-start.24 = (f32[2,3,16,128]{3,2,1,0:T(8,128)S(1)}, f32[2,3,16,128]{3,2,1,0:T(8,128)S(1)}, u32[]{:S(2)}, u32[]{:S(2)}) collective-permute-start(f32[2,3,16,128]{3,2,1,0:T(8,128)S(1)} %fusion.58), channel_id=1, source_target_pairs={{0,2},{1,3},{2,4},{3,5},{4,6},{5,7},{8,10},{9,11},{10,12},{11,13},... | collective-permute-start | bytes 147464 | tf_op jit(solution)/shard_map/ppermute | solution.py:23
  115.1 6.2 %collective-permute-done.18 = f32[4,16,128]{2,1,0:T(8,128)S(1)} collective-permute-done((f32[4,16,128]{2,1,0:T(8,128)S(1)}, f32[4,16,128]{2,1,0:T(8,128)S(1)}, u32[]{:S(2)}, u32[]{:S(2)}) %collective-permute-start.18) | collective-permute-done | bytes 32800 | tf_op jit(solution)/shard_map/ppermute | solution.py:23
  121.4 5.0 %collective-permute-start.26 = (f32[2,3,16,128]{3,2,1,0:T(8,128)S(1)}, f32[2,3,16,128]{3,2,1,0:T(8,128)S(1)}, u32[]{:S(2)}, u32[]{:S(2)}) collective-permute-start(f32[2,3,16,128]{3,2,1,0:T(8,128)S(1)} %fusion.59), channel_id=1, source_target_pairs={{0,4},{1,5},{2,6},{3,7},{8,12},{9,13},{10,14},{11,15},{16,20},{17,... | collective-permute-start | bytes 147464 | tf_op jit(solution)/shard_map/ppermute | solution.py:23
  127.8 8.5 %collective-permute-start.19 = (f32[4,16,128]{2,1,0:T(8,128)S(1)}, f32[4,16,128]{2,1,0:T(8,128)S(1)}, u32[]{:S(2)}, u32[]{:S(2)}) collective-permute-start(f32[4,16,128]{2,1,0:T(8,128)S(1)} %pad_maximum_fusion.60), channel_id=1, source_target_pairs={{0,4},{1,5},{2,6},{3,7},{8,12},{9,13},{10,14},{11,15},{16,20},{17,... | collective-permute-start | bytes 98312 | tf_op jit(solution)/shard_map/ppermute | solution.py:23
  137.9 8.1 %collective-permute-done.21 = f32[4,16,128]{2,1,0:T(8,128)S(1)} collective-permute-done((f32[4,16,128]{2,1,0:T(8,128)S(1)}, f32[4,16,128]{2,1,0:T(8,128)S(1)}, u32[]{:S(2)}, u32[]{:S(2)}) %collective-permute-start.21) | collective-permute-done | bytes 32800 | tf_op jit(solution)/shard_map/ppermute | solution.py:23
  159.3 4.0 %collective-permute-done.30 = f32[3,16,18,1]{2,1,3,0:T(8,128)} collective-permute-done((f32[3,16,18,1]{2,1,3,0:T(8,128)S(1)}, f32[3,16,18,1]{2,1,3,0:T(8,128)}, u32[]{:S(2)}, u32[]{:S(2)}) %collective-permute-start.30) | collective-permute-done | bytes 3488 | tf_op jit(solution)/shard_map/ppermute | solution.py:14
  167.3 4.1 %collective-permute-start.33 = (f32[3,1,18,130]{3,2,0,1:T(8,128)S(1)}, f32[3,1,18,130]{3,2,0,1:T(8,128)S(1)}, u32[]{:S(2)}, u32[]{:S(2)}) collective-permute-start(f32[3,1,18,130]{3,2,0,1:T(8,128)S(1)} %get-tuple-element.85), channel_id=1, source_target_pairs={{1,0},{2,1},{3,2},{4,3},{5,4},{6,5},{7,6},{9,8},{10,9},{11,10},{12... | collective-permute-start | bytes 84248 | tf_op jit(solution)/shard_map/ppermute | solution.py:15
  179.6 3.4 %collective-permute-start.35 = (f32[2,3,16,128]{3,2,1,0:T(8,128)S(1)}, f32[2,3,16,128]{3,2,1,0:T(8,128)S(1)}, u32[]{:S(2)}, u32[]{:S(2)}) collective-permute-start(f32[2,3,16,128]{3,2,1,0:T(8,128)S(1)} %pad_maximum_fusion.54), channel_id=1, source_target_pairs={{1,0},{2,1},{3,2},{4,3},{5,4},{6,5},{7,6},{9,8},{10,9},{11,10},{12... | collective-permute-start | bytes 147464 | tf_op jit(solution)/shard_map/ppermute | solution.py:23
  185.6 3.8 %collective-permute-start.36 = (f32[2,3,16,128]{3,2,1,0:T(8,128)S(1)}, f32[2,3,16,128]{3,2,1,0:T(8,128)S(1)}, u32[]{:S(2)}, u32[]{:S(2)}) collective-permute-start(f32[2,3,16,128]{3,2,1,0:T(8,128)S(1)} %fusion.61), channel_id=1, source_target_pairs={{0,2},{1,3},{2,4},{3,5},{4,6},{5,7},{8,10},{9,11},{10,12},{11,13},... | collective-permute-start | bytes 147464 | tf_op jit(solution)/shard_map/ppermute | solution.py:23
  191.6 5.1 %collective-permute-done.37 = f32[2,3,16,128]{3,2,1,0:T(8,128)S(1)} collective-permute-done((f32[2,3,16,128]{3,2,1,0:T(8,128)S(1)}, f32[2,3,16,128]{3,2,1,0:T(8,128)S(1)}, u32[]{:S(2)}, u32[]{:S(2)}) %collective-permute-start.37) | collective-permute-done | bytes 49184 | tf_op jit(solution)/shard_map/ppermute | solution.py:23
  200.6 8.3 %collective-permute-done.39 = f32[2,3,16,128]{3,2,1,0:T(8,128)S(1)} collective-permute-done((f32[2,3,16,128]{3,2,1,0:T(8,128)S(1)}, f32[2,3,16,128]{3,2,1,0:T(8,128)S(1)}, u32[]{:S(2)}, u32[]{:S(2)}) %collective-permute-start.39) | collective-permute-done | bytes 49184 | tf_op jit(solution)/shard_map/ppermute | solution.py:23
  221.6 4.0 %collective-permute-done.42 = f32[3,16,18,1]{2,1,3,0:T(8,128)S(1)} collective-permute-done((f32[3,16,18,1]{2,1,3,0:T(8,128)S(1)}, f32[3,16,18,1]{2,1,3,0:T(8,128)S(1)}, u32[]{:S(2)}, u32[]{:S(2)}) %collective-permute-start.42) | collective-permute-done | bytes 3488 | tf_op jit(solution)/shard_map/ppermute | solution.py:14
  (451 shorter events, 103.9 us)
Async XLA Ops:
  36.6 7.0 %collective-permute-start.8 = (f32[4,16,128]{2,1,0:T(8,128)S(1)}, f32[4,16,128]{2,1,0:T(8,128)S(1)}, u32[]{:S(2)}, u32[]{:S(2)}) collective-permute-start(f32[4,16,128]{2,1,0:T(8,128)S(1)} %pad_maximum_fusion.55), channel_id=1, source_target_pairs={{1,0},{2,1},{3,2},{4,3},{5,4},{6,5},{7,6},{9,8},{10,9},{11,10},{12... | collective-permute-start | bytes 98312 | tf_op jit(solution)/shard_map/ppermute | solution.py:23
  45.2 13.8 %collective-permute-start.9 = (f32[4,16,128]{2,1,0:T(8,128)S(1)}, f32[4,16,128]{2,1,0:T(8,128)S(1)}, u32[]{:S(2)}, u32[]{:S(2)}) collective-permute-start(f32[4,16,128]{2,1,0:T(8,128)S(1)} %get-tuple-element.335), channel_id=1, source_target_pairs={{1,0},{2,1},{3,2},{4,3},{5,4},{6,5},{7,6},{9,8},{10,9},{11,10},{12... | collective-permute-start | bytes 98312 | tf_op jit(solution)/shard_map/ppermute | solution.py:23
  47.1 34.1 %collective-permute-start.10 = (f32[4,16,128]{2,1,0:T(8,128)S(1)}, f32[4,16,128]{2,1,0:T(8,128)S(1)}, u32[]{:S(2)}, u32[]{:S(2)}) collective-permute-start(f32[4,16,128]{2,1,0:T(8,128)S(1)} %get-tuple-element.335), channel_id=1, source_target_pairs={{0,1},{1,2},{2,3},{3,4},{4,5},{5,6},{6,7},{8,9},{9,10},{10,11},{11... | collective-permute-start | bytes 98312 | tf_op jit(solution)/shard_map/ppermute | solution.py:23
  52.2 6.7 %collective-permute-start.7 = (f32[4,16,128]{2,1,0:T(8,128)S(1)}, f32[4,16,128]{2,1,0:T(8,128)S(1)}, u32[]{:S(2)}, u32[]{:S(2)}) collective-permute-start(f32[4,16,128]{2,1,0:T(8,128)S(1)} %get-tuple-element.336), channel_id=1, source_target_pairs={{0,1},{1,2},{2,3},{3,4},{4,5},{5,6},{6,7},{8,9},{9,10},{10,11},{11... | collective-permute-start | bytes 98312 | tf_op jit(solution)/shard_map/ppermute | solution.py:23
  59.0 16.2 %collective-permute-start.14 = (f32[4,16,128]{2,1,0:T(8,128)S(1)}, f32[4,16,128]{2,1,0:T(8,128)S(1)}, u32[]{:S(2)}, u32[]{:S(2)}) collective-permute-start(f32[4,16,128]{2,1,0:T(8,128)S(1)} %fusion.64), channel_id=1, source_target_pairs={{2,0},{3,1},{4,2},{5,3},{6,4},{7,5},{10,8},{11,9},{12,10},{13,11},... | collective-permute-start | bytes 98312 | tf_op jit(solution)/shard_map/ppermute | solution.py:23
  60.3 16.9 %collective-permute-start.11 = (f32[4,16,128]{2,1,0:T(8,128)S(1)}, f32[4,16,128]{2,1,0:T(8,128)S(1)}, u32[]{:S(2)}, u32[]{:S(2)}) collective-permute-start(f32[4,16,128]{2,1,0:T(8,128)S(1)} %fusion.64), channel_id=1, source_target_pairs={{0,2},{1,3},{2,4},{3,5},{4,6},{5,7},{8,10},{9,11},{10,12},{11,13},... | collective-permute-start | bytes 98312 | tf_op jit(solution)/shard_map/ppermute | solution.py:23
  68.5 27.1 %collective-permute-start.22 = (f32[2,3,16,128]{3,2,1,0:T(8,128)S(1)}, f32[2,3,16,128]{3,2,1,0:T(8,128)S(1)}, u32[]{:S(2)}, u32[]{:S(2)}) collective-permute-start(f32[2,3,16,128]{3,2,1,0:T(8,128)S(1)} %pad_maximum_fusion.53), channel_id=1, source_target_pairs={{0,1},{1,2},{2,3},{3,4},{4,5},{5,6},{6,7},{8,9},{9,10},{10,11},{11... | collective-permute-start | bytes 147464 | tf_op jit(solution)/shard_map/ppermute | solution.py:23
  73.3 22.3 %collective-permute-start.23 = (f32[2,3,16,128]{3,2,1,0:T(8,128)S(1)}, f32[2,3,16,128]{3,2,1,0:T(8,128)S(1)}, u32[]{:S(2)}, u32[]{:S(2)}) collective-permute-start(f32[2,3,16,128]{3,2,1,0:T(8,128)S(1)} %pad_maximum_fusion.53), channel_id=1, source_target_pairs={{1,0},{2,1},{3,2},{4,3},{5,4},{6,5},{7,6},{9,8},{10,9},{11,10},{12... | collective-permute-start | bytes 147464 | tf_op jit(solution)/shard_map/ppermute | solution.py:23
  81.2 16.0 %collective-permute-start.15 = (f32[4,16,128]{2,1,0:T(8,128)S(1)}, f32[4,16,128]{2,1,0:T(8,128)S(1)}, u32[]{:S(2)}, u32[]{:S(2)}) collective-permute-start(f32[4,16,128]{2,1,0:T(8,128)S(1)} %pad_maximum_fusion.59), channel_id=1, source_target_pairs={{2,0},{3,1},{4,2},{5,3},{6,4},{7,5},{10,8},{11,9},{12,10},{13,11},... | collective-permute-start | bytes 98312 | tf_op jit(solution)/shard_map/ppermute | solution.py:23
  82.5 32.4 %collective-permute-start.16 = (f32[4,16,128]{2,1,0:T(8,128)S(1)}, f32[4,16,128]{2,1,0:T(8,128)S(1)}, u32[]{:S(2)}, u32[]{:S(2)}) collective-permute-start(f32[4,16,128]{2,1,0:T(8,128)S(1)} %pad_maximum_fusion.59), channel_id=1, source_target_pairs={{0,2},{1,3},{2,4},{3,5},{4,6},{5,7},{8,10},{9,11},{10,12},{11,13},... | collective-permute-start | bytes 98312 | tf_op jit(solution)/shard_map/ppermute | solution.py:23
  89.6 7.6 %collective-permute-start.13 = (f32[4,16,128]{2,1,0:T(8,128)S(1)}, f32[4,16,128]{2,1,0:T(8,128)S(1)}, u32[]{:S(2)}, u32[]{:S(2)}) collective-permute-start(f32[4,16,128]{2,1,0:T(8,128)S(1)} %pad_maximum_fusion.58), channel_id=1, source_target_pairs={{0,2},{1,3},{2,4},{3,5},{4,6},{5,7},{8,10},{9,11},{10,12},{11,13},... | collective-permute-start | bytes 98312 | tf_op jit(solution)/shard_map/ppermute | solution.py:23
  97.3 16.2 %collective-permute-start.20 = (f32[4,16,128]{2,1,0:T(8,128)S(1)}, f32[4,16,128]{2,1,0:T(8,128)S(1)}, u32[]{:S(2)}, u32[]{:S(2)}) collective-permute-start(f32[4,16,128]{2,1,0:T(8,128)S(1)} %fusion.65), channel_id=1, source_target_pairs={{4,0},{5,1},{6,2},{7,3},{12,8},{13,9},{14,10},{15,11},{20,16},{21,... | collective-permute-start | bytes 98312 | tf_op jit(solution)/shard_map/ppermute | solution.py:23
  98.6 16.3 %collective-permute-start.17 = (f32[4,16,128]{2,1,0:T(8,128)S(1)}, f32[4,16,128]{2,1,0:T(8,128)S(1)}, u32[]{:S(2)}, u32[]{:S(2)}) collective-permute-start(f32[4,16,128]{2,1,0:T(8,128)S(1)} %fusion.65), channel_id=1, source_target_pairs={{0,4},{1,5},{2,6},{3,7},{8,12},{9,13},{10,14},{11,15},{16,20},{17,... | collective-permute-start | bytes 98312 | tf_op jit(solution)/shard_map/ppermute | solution.py:23
  107.0 8.0 %collective-permute-start.24 = (f32[2,3,16,128]{3,2,1,0:T(8,128)S(1)}, f32[2,3,16,128]{3,2,1,0:T(8,128)S(1)}, u32[]{:S(2)}, u32[]{:S(2)}) collective-permute-start(f32[2,3,16,128]{3,2,1,0:T(8,128)S(1)} %fusion.58), channel_id=1, source_target_pairs={{0,2},{1,3},{2,4},{3,5},{4,6},{5,7},{8,10},{9,11},{10,12},{11,13},... | collective-permute-start | bytes 147464 | tf_op jit(solution)/shard_map/ppermute | solution.py:23
  112.2 9.1 %collective-permute-start.25 = (f32[2,3,16,128]{3,2,1,0:T(8,128)S(1)}, f32[2,3,16,128]{3,2,1,0:T(8,128)S(1)}, u32[]{:S(2)}, u32[]{:S(2)}) collective-permute-start(f32[2,3,16,128]{3,2,1,0:T(8,128)S(1)} %fusion.58), channel_id=1, source_target_pairs={{2,0},{3,1},{4,2},{5,3},{6,4},{7,5},{10,8},{11,9},{12,10},{13,11},... | collective-permute-start | bytes 147464 | tf_op jit(solution)/shard_map/ppermute | solution.py:23
  113.5 7.8 %collective-permute-start.18 = (f32[4,16,128]{2,1,0:T(8,128)S(1)}, f32[4,16,128]{2,1,0:T(8,128)S(1)}, u32[]{:S(2)}, u32[]{:S(2)}) collective-permute-start(f32[4,16,128]{2,1,0:T(8,128)S(1)} %pad_maximum_fusion.58), channel_id=1, source_target_pairs={{2,0},{3,1},{4,2},{5,3},{6,4},{7,5},{10,8},{11,9},{12,10},{13,11},... | collective-permute-start | bytes 98312 | tf_op jit(solution)/shard_map/ppermute | solution.py:23
  121.4 24.8 %collective-permute-start.26 = (f32[2,3,16,128]{3,2,1,0:T(8,128)S(1)}, f32[2,3,16,128]{3,2,1,0:T(8,128)S(1)}, u32[]{:S(2)}, u32[]{:S(2)}) collective-permute-start(f32[2,3,16,128]{3,2,1,0:T(8,128)S(1)} %fusion.59), channel_id=1, source_target_pairs={{0,4},{1,5},{2,6},{3,7},{8,12},{9,13},{10,14},{11,15},{16,20},{17,... | collective-permute-start | bytes 147464 | tf_op jit(solution)/shard_map/ppermute | solution.py:23
  126.4 19.8 %collective-permute-start.27 = (f32[2,3,16,128]{3,2,1,0:T(8,128)S(1)}, f32[2,3,16,128]{3,2,1,0:T(8,128)S(1)}, u32[]{:S(2)}, u32[]{:S(2)}) collective-permute-start(f32[2,3,16,128]{3,2,1,0:T(8,128)S(1)} %fusion.59), channel_id=1, source_target_pairs={{4,0},{5,1},{6,2},{7,3},{12,8},{13,9},{14,10},{15,11},{20,16},{21,... | collective-permute-start | bytes 147464 | tf_op jit(solution)/shard_map/ppermute | solution.py:23
  127.8 10.0 %collective-permute-start.19 = (f32[4,16,128]{2,1,0:T(8,128)S(1)}, f32[4,16,128]{2,1,0:T(8,128)S(1)}, u32[]{:S(2)}, u32[]{:S(2)}) collective-permute-start(f32[4,16,128]{2,1,0:T(8,128)S(1)} %pad_maximum_fusion.60), channel_id=1, source_target_pairs={{0,4},{1,5},{2,6},{3,7},{8,12},{9,13},{10,14},{11,15},{16,20},{17,... | collective-permute-start | bytes 98312 | tf_op jit(solution)/shard_map/ppermute | solution.py:23
  136.3 9.7 %collective-permute-start.21 = (f32[4,16,128]{2,1,0:T(8,128)S(1)}, f32[4,16,128]{2,1,0:T(8,128)S(1)}, u32[]{:S(2)}, u32[]{:S(2)}) collective-permute-start(f32[4,16,128]{2,1,0:T(8,128)S(1)} %pad_maximum_fusion.61), channel_id=1, source_target_pairs={{4,0},{5,1},{6,2},{7,3},{12,8},{13,9},{14,10},{15,11},{20,16},{21,... | collective-permute-start | bytes 98312 | tf_op jit(solution)/shard_map/ppermute | solution.py:23
  165.4 6.6 %collective-permute-start.32 = (f32[3,1,18,130]{3,2,0,1:T(8,128)S(1)}, f32[3,1,18,130]{3,2,0,1:T(8,128)S(1)}, u32[]{:S(2)}, u32[]{:S(2)}) collective-permute-start(f32[3,1,18,130]{3,2,0,1:T(8,128)S(1)} %get-tuple-element.84), channel_id=1, source_target_pairs={{0,1},{1,2},{2,3},{3,4},{4,5},{5,6},{6,7},{8,9},{9,10},{10,11},{11... | collective-permute-start | bytes 84248 | tf_op jit(solution)/shard_map/ppermute | solution.py:14
  189.4 7.3 %collective-permute-start.37 = (f32[2,3,16,128]{3,2,1,0:T(8,128)S(1)}, f32[2,3,16,128]{3,2,1,0:T(8,128)S(1)}, u32[]{:S(2)}, u32[]{:S(2)}) collective-permute-start(f32[2,3,16,128]{3,2,1,0:T(8,128)S(1)} %fusion.61), channel_id=1, source_target_pairs={{2,0},{3,1},{4,2},{5,3},{6,4},{7,5},{10,8},{11,9},{12,10},{13,11},... | collective-permute-start | bytes 147464 | tf_op jit(solution)/shard_map/ppermute | solution.py:23
  198.6 10.2 %collective-permute-start.39 = (f32[2,3,16,128]{3,2,1,0:T(8,128)S(1)}, f32[2,3,16,128]{3,2,1,0:T(8,128)S(1)}, u32[]{:S(2)}, u32[]{:S(2)}) collective-permute-start(f32[2,3,16,128]{3,2,1,0:T(8,128)S(1)} %fusion.62), channel_id=1, source_target_pairs={{4,0},{5,1},{6,2},{7,3},{12,8},{13,9},{14,10},{15,11},{20,16},{21,... | collective-permute-start | bytes 147464 | tf_op jit(solution)/shard_map/ppermute | solution.py:23
  226.7 7.2 %collective-permute-start.45 = (f32[3,1,18,130]{3,1,2,0:T(1,128)S(1)}, f32[3,1,18,130]{3,1,2,0:T(1,128)S(1)}, u32[]{:S(2)}, u32[]{:S(2)}) collective-permute-start(f32[3,1,18,130]{3,1,2,0:T(1,128)S(1)} %get-tuple-element.87), channel_id=1, source_target_pairs={{1,0},{2,1},{3,2},{4,3},{5,4},{6,5},{7,6},{9,8},{10,9},{11,10},{12... | collective-permute-start | bytes 84248 | tf_op jit(solution)/shard_map/ppermute | solution.py:15
  (106 other events, 1776.0 us)
where the time goes:
time: 239 us; the launch traced here: 237 us
  starting transfers between devices  141 us (59%)
  waiting for transfers between devices  66.5 us (28%)
  local copies, waits for them, and re-layouts  15 us (6%)
  other arithmetic  11.4 us (5%)
  between operations  3.46 us (1%)
    ppermute x28, starting transfers between devices, from_behind(): return lax.ppermute(block, axis, route)  99 us
    ppermute x28, waiting for transfers between devices, from_behind(): return lax.ppermute(block, axis, route)  40.2 us
    ppermute x9, starting transfers between devices, with_halo(): after = lax.ppermute(leading, axis, down)  22.3 us
    ppermute x9, waiting for transfers between devices, with_halo(): before = lax.ppermute(last, axis, up)  21.3 us
    ppermute x9, starting transfers between devices, with_halo(): before = lax.ppermute(last, axis, up)  19.8 us
    unnamed x180, local copies, waits for them, and re-layouts  5.48 us
    ppermute x9, waiting for transfers between devices, with_halo(): after = lax.ppermute(leading, axis, down)  4.94 us
  transfers between devices with their start and end apart: 46, of which 23 were waited for; matrix products, arithmetic and copies ran while one was open for 3% of the time, Pallas kernels for 0%

commit v1 on v0

v1 whole, which is shorter than its diff:
```python
import jax
import jax.numpy as jnp
from jax import lax
from jax.sharding import PartitionSpec as P


def from_prev(block, axis):
    size = lax.axis_size(axis)
    return lax.ppermute(block, axis, [(i, i + 1) for i in range(size - 1)])


def from_next(block, axis):
    size = lax.axis_size(axis)
    return lax.ppermute(block, axis, [(i + 1, i) for i in range(size - 1)])


def neighbours(values, axis, dim):
    n = values.shape[dim]
    low = from_prev(lax.slice_in_dim(values, n - 1, n, axis=dim), axis)
    high = from_next(lax.slice_in_dim(values, 0, 1, axis=dim), axis)
    below = jnp.concatenate([low, lax.slice_in_dim(values, 0, n - 1, axis=dim)], dim)
    above = jnp.concatenate([lax.slice_in_dim(values, 1, n, axis=dim), high], dim)
    return below, above


def shifted(values, low, high, dim):
    n = values.shape[dim]
    below = jnp.concatenate([low, lax.slice_in_dim(values, 0, n - 1, axis=dim)], dim)
    above = jnp.concatenate([lax.slice_in_dim(values, 1, n, axis=dim), high], dim)
    return below, above


def face_pair(centre, beside):
    inside = beside > 0.0
    harmonic = 2.0 * centre * beside / (centre + beside)
    return (
        jnp.where(inside, harmonic, 2.0 * centre),
        jnp.where(inside, harmonic, centre),
        jnp.where(inside, harmonic, 0.0),
    )


def table_lookup(facies, perm_table):
    perm = jnp.zeros((3,) + facies.shape, jnp.float32)
    for label in range(perm_table.shape[1]):
        perm = jnp.where((facies == label)[None], perm_table[:, label][:, None, None, None], perm)
    return perm


def shift_rows(values, stride, fill, axis):
    count = values.shape[axis]
    step = abs(stride)
    filler = jnp.full_like(lax.slice_in_dim(values, 0, step, axis=axis), fill)
    if stride > 0:
        return jnp.concatenate([filler, lax.slice_in_dim(values, 0, count - step, axis=axis)], axis)
    return jnp.concatenate([lax.slice_in_dim(values, step, count, axis=axis), filler], axis)


def interior_solve(sub_diag, main_diag, super_diag, columns):
    stride = 1
    count = main_diag.shape[0]
    while stride < count:
        sub_low = shift_rows(sub_diag, stride, 0.0, 0)
        super_low = shift_rows(super_diag, stride, 0.0, 0)
        main_low = shift_rows(main_diag, stride, 1.0, 0)
        column_low = shift_rows(columns, stride, 0.0, 1)
        sub_high = shift_rows(sub_diag, -stride, 0.0, 0)
        super_high = shift_rows(super_diag, -stride, 0.0, 0)
        main_high = shift_rows(main_diag, -stride, 1.0, 0)
        column_high = shift_rows(columns, -stride, 0.0, 1)
        left = sub_diag / main_low
        right = super_diag / main_high
        main_diag = main_diag - left * super_low - right * sub_high
        columns = columns - left[None] * column_low - right[None] * column_high
        sub_diag = -left * sub_low
        super_diag = -right * super_high
        stride *= 2
    return columns / main_diag[None]


def lateral_sides(field):
    x_low, x_high = neighbours(field, "gx", 2)
    y_low, y_high = neighbours(field, "gy", 3)
    return x_low, x_high, y_low, y_high


def per_device(facies, perm_table, line_breaks):
    depth = facies.shape[0]
    inner = depth - 2
    count = lax.axis_size("gz")
    position = lax.axis_index("gz")
    perm = table_lookup(facies, perm_table)
    px, py, pz = perm[0], perm[1], perm[2]
    z_below, z_above = neighbours(pz, "gz", 0)
    x_below, x_above = neighbours(px, "gx", 1)
    y_below, y_above = neighbours(py, "gy", 2)
    z_low = face_pair(pz, z_below)
    z_high = face_pair(pz, z_above)
    x_low = face_pair(px, x_below)
    x_high = face_pair(px, x_above)
    y_low = face_pair(py, y_below)
    y_high = face_pair(py, y_above)
    taus = (z_low[0], z_high[0], x_low[0], x_high[0], y_low[0], y_high[0])
    source = jnp.stack([x_high[1] - x_low[1], y_high[1] - y_low[1], z_high[1] - z_low[1]])
    centre_sum = taus[0] + taus[1] + taus[2] + taus[3] + taus[4] + taus[5]
    link_low, link_high = z_low[2], z_high[2]

    extended = jnp.concatenate(
        [jnp.zeros((1,), jnp.int32), line_breaks, jnp.zeros((1,), jnp.int32)]
    ).astype(jnp.float32)
    window = lax.dynamic_slice_in_dim(extended, position * depth, depth + 1)
    break_low = window[:depth][:, None, None]
    break_high = window[1:][:, None, None]
    sub_diag = -link_low * (1.0 - break_low)
    super_diag = -link_high * (1.0 - break_high)
    single_row = jnp.zeros_like(sub_diag[1:2])
    blank = jnp.zeros((inner - 1,) + sub_diag.shape[1:], jnp.float32)
    inner_sub = jnp.concatenate([single_row, sub_diag[2 : depth - 1]])
    inner_super = jnp.concatenate([super_diag[1 : depth - 2], single_row])
    inner_main = centre_sum[1 : depth - 1]
    push_low = jnp.concatenate([-sub_diag[1:2], blank])
    push_high = jnp.concatenate([blank, -super_diag[depth - 2 : depth - 1]])
    columns = jnp.concatenate([source[:, 1 : depth - 1], push_low[None], push_high[None]])
    solved = interior_solve(inner_sub, inner_main, inner_super, columns)
    inner_first = solved[:3]
    weight_low = solved[3]
    weight_high = solved[4]
    lower_u = sub_diag[0]
    centre_u = centre_sum[0] + super_diag[0] * weight_low[0]
    upper_u = super_diag[0] * weight_high[0]
    lower_v = sub_diag[depth - 1] * weight_low[inner - 1]
    centre_v = centre_sum[depth - 1] + sub_diag[depth - 1] * weight_high[inner - 1]
    upper_v = super_diag[depth - 1]

    def reduced_source(right, interior):
        return jnp.stack(
            [
                right[:, 0] - super_diag[0][None] * interior[:, 0],
                right[:, depth - 1] - sub_diag[depth - 1][None] * interior[:, inner - 1],
            ]
        )

    def rebuild(interior, ends):
        middle = (
            interior + weight_low[None] * ends[0][:, None] + weight_high[None] * ends[1][:, None]
        )
        return jnp.concatenate([ends[0][:, None], middle, ends[1][:, None]], axis=1)

    coefficients = jnp.stack([lower_u, centre_u, upper_u, lower_v, centre_v, upper_v])
    pair_first = reduced_source(source, inner_first)
    packed = jnp.concatenate([coefficients, pair_first.reshape((6,) + lower_u.shape)])
    gathered = lax.all_gather(packed, "gz")
    lower, diag, upper = [], [], []
    for k in range(count):
        lower += [gathered[k, 0], gathered[k, 3]]
        diag += [gathered[k, 1], gathered[k, 4]]
        upper += [gathered[k, 2], gathered[k, 5]]
    unknowns = 2 * count
    pivots, ratios = [], []
    for i in range(unknowns):
        pivot = diag[i] if i == 0 else diag[i] - lower[i] * ratios[i - 1]
        pivots.append(pivot)
        ratios.append(upper[i] / pivot)

    def reduced_solve(rhs):
        partial = []
        for i in range(unknowns):
            value = rhs[i] if i == 0 else rhs[i] - lower[i][None] * partial[i - 1]
            partial.append(value / pivots[i][None])
        result = [None] * unknowns
        result[unknowns - 1] = partial[unknowns - 1]
        for i in range(unknowns - 2, -1, -1):
            result[i] = partial[i] - ratios[i][None] * result[i + 1]
        zero = jnp.zeros_like(result[0])
        padded = jnp.stack([zero] + result + [zero])
        return lax.dynamic_slice_in_dim(padded, 2 * position, 4)

    def rhs_list(pairs):
        values = []
        for k in range(count):
            values += [pairs[k, 0], pairs[k, 1]]
        return values

    ends_first = reduced_solve(rhs_list(gathered[:, 6:].reshape((count, 2, 3) + lower_u.shape)))
    first = rebuild(inner_first, ends_first[1:3])
    f_z_low, f_z_high = shifted(first, ends_first[0][:, None], ends_first[3][:, None], 1)
    f_x_low, f_x_high, f_y_low, f_y_high = lateral_sides(first)
    right = source + (
        taus[2] * f_x_low
        + taus[3] * f_x_high
        + taus[4] * f_y_low
        + taus[5] * f_y_high
        + taus[0] * break_low * f_z_low
        + taus[1] * break_high * f_z_high
    )
    inner_second = interior_solve(inner_sub, inner_main, inner_super, right[:, 1 : depth - 1])
    pair_second = reduced_source(right, inner_second)
    gathered_second = lax.all_gather(pair_second, "gz")
    ends_second = reduced_solve(rhs_list(gathered_second))
    second = rebuild(inner_second, ends_second[1:3])
    s_z_low, s_z_high = shifted(second, ends_second[0][:, None], ends_second[3][:, None], 1)
    s_x_low, s_x_high, s_y_low, s_y_high = lateral_sides(second)
    total = (
        taus[0] * s_z_low
        + taus[1] * s_z_high
        + taus[2] * s_x_low
        + taus[3] * s_x_high
        + taus[4] * s_y_low
        + taus[5] * s_y_high
    )
    residual = source - centre_sum * second + total
    return (second, residual)


def solution(mesh):
    return jax.shard_map(
        per_device,
        mesh=mesh,
        in_specs=(P("gz", "gx", "gy"), P(), P()),
        out_specs=(P(None, "gz", "gx", "gy"), P(None, "gz", "gx", "gy")),
        check_vma=False,
    )
```

time: 239 us -> 114 us (0.48)
  the two profiles are of different devices: /device:TPU:62 before, /device:TPU:1 now
where the time goes in v1:
time: 114 us; the launch traced here: 113 us
  starting transfers between devices  51.2 us (45%)
  blocking collectives  42.9 us (38%)
  other arithmetic  6.21 us (5%)
  waiting for transfers between devices  6.19 us (5%)
  local copies, waits for them, and re-layouts  4.68 us (4%)
  between operations  1.63 us (1%)
    ppermute x7, starting transfers between devices, from_prev(): return lax.ppermute(block, axis, [(i, i + 1) for i in range(size - 1)])  37.1 us
    all_gather x1, blocking collectives, per_device(): gathered = lax.all_gather(packed, 'gz')  24.1 us
    all_gather x1, blocking collectives, per_device(): gathered_second = lax.all_gather(pair_second, 'gz')  18.8 us
    ppermute x7, starting transfers between devices, from_next(): return lax.ppermute(block, axis, [(i + 1, i) for i in range(size - 1)])  14 us
    ppermute x7, waiting for transfers between devices, from_next(): return lax.ppermute(block, axis, [(i + 1, i) for i in range(size - 1)])  5.46 us
    unnamed x23, local copies, waits for them, and re-layouts  2.29 us
  transfers between devices with their start and end apart: 14, of which 3 were waited for; matrix products, arithmetic and copies ran while one was open for 1% of the time, Pallas kernels for 0%

profile of v1, /device:TPU:1, one launch (start us, length us, event | category | flops | bytes accessed | tf_op | source)
XLA Modules:
  0.0 112.8 jit_solution(10840264579094083108)
XLA Ops:
  0.6 1.2 %broadcast_compare_fusion.17 = (pred[16,16,128]{2,1,0:T(8,128)(4,1)S(1)}, pred[16,16,128]{2,1,0:T(8,128)(4,1)S(1)}, pred[16,16,128]{2,1,0:T(8,128)(4,1)S(1)}, pr...) fusion(s32[16,16,128]{2,1,0:T(8,128)} %param.3), kind=kLoop, calls=%fused_computation.184 | loop fusion | flops 524288 | bytes 655360 | tf_op jit(solution)/shard_map/eq | solution.py:46
  2.9 1.3 %collective-permute-start.2 = (f32[16,16,1]{2,1,0:T(8,128)S(1)}, f32[16,16,1]{2,1,0:T(8,128)S(1)}, u32[]{:S(2)}, u32[]{:S(2)}) collective-permute-start(f32[16,16,1]{2,1,0:T(8,128)S(1)} %get-tuple-element.220), channel_id=1, source_target_pairs={{8,0},{16,8},{24,16},{9,1},{17,9},{25,17},{10,2},{18,10},{26,18},{... | collective-permute-start | bytes 3080 | tf_op jit(solution)/shard_map/ppermute | solution.py:14
  4.2 4.7 %collective-permute-start.3 = (f32[16,16,1]{2,1,0:T(8,128)S(1)}, f32[16,16,1]{2,1,0:T(8,128)S(1)}, u32[]{:S(2)}, u32[]{:S(2)}) collective-permute-start(f32[16,16,1]{2,1,0:T(8,128)S(1)} %get-tuple-element.219), channel_id=1, source_target_pairs={{0,8},{8,16},{16,24},{1,9},{9,17},{17,25},{2,10},{10,18},{18,26},{... | collective-permute-start | bytes 3080 | tf_op jit(solution)/shard_map/ppermute | solution.py:9
  8.9 5.0 %collective-permute-start = (f32[16,1,128]{2,1,0:T(1,128)S(1)}, f32[16,1,128]{2,1,0:T(1,128)S(1)}, u32[]{:S(2)}, u32[]{:S(2)}) collective-permute-start(f32[16,1,128]{2,1,0:T(1,128)S(1)} %get-tuple-element.218), channel_id=1, source_target_pairs={{32,0},{64,32},{96,64},{128,96},{160,128},{192,160},{224,192},{33,... | collective-permute-start | bytes 24584 | tf_op jit(solution)/shard_map/ppermute | solution.py:14
  14.0 1.9 %collective-permute-start.1 = (f32[16,1,128]{2,1,0:T(1,128)S(1)}, f32[16,1,128]{2,1,0:T(1,128)S(1)}, u32[]{:S(2)}, u32[]{:S(2)}) collective-permute-start(f32[16,1,128]{2,1,0:T(1,128)S(1)} %get-tuple-element.217), channel_id=1, source_target_pairs={{0,32},{32,64},{64,96},{96,128},{128,160},{160,192},{192,224},{1,3... | collective-permute-start | bytes 24584 | tf_op jit(solution)/shard_map/ppermute | solution.py:9
  15.9 1.3 %collective-permute-start.4 = (f32[1,16,128]{2,1,0:T(8,128)S(1)}, f32[1,16,128]{2,1,0:T(8,128)S(1)}, u32[]{:S(2)}, u32[]{:S(2)}) collective-permute-start(f32[1,16,128]{2,1,0:T(8,128)S(1)} %get-tuple-element.192), channel_id=1, source_target_pairs={{1,0},{2,1},{3,2},{4,3},{5,4},{6,5},{7,6},{9,8},{10,9},{11,10},{12... | collective-permute-start | bytes 24584 | tf_op jit(solution)/shard_map/ppermute | solution.py:14
  17.4 0.6 copy-done.1
  18.3 4.0 %collective-permute-start.5 = (f32[1,16,128]{2,1,0:T(8,128)S(1)}, f32[1,16,128]{2,1,0:T(8,128)S(1)}, u32[]{:S(2)}, u32[]{:S(2)}) collective-permute-start(f32[1,16,128]{2,1,0:T(8,128)S(1)} %get-tuple-element.191), channel_id=1, source_target_pairs={{0,1},{1,2},{2,3},{3,4},{4,5},{5,6},{6,7},{8,9},{9,10},{10,11},{11... | collective-permute-start | bytes 24584 | tf_op jit(solution)/shard_map/ppermute | solution.py:9
  22.4 0.7 collective-permute-done.5
  25.9 24.1 %all-gather = f32[96,16,128]{2,1,0:T(8,128)S(1)} all-gather(f32[12,16,128]{2,1,0:T(8,128)S(1)} %constant_dynamic-update-slice_fusion), channel_id=2, replica_groups=mesh['gx'=8,'gy'=4,'gz'=8] {'gz'}, dimensions={0}, use_global_device_ids=true | all-gather | bytes 884736 | tf_op jit(solution)/shard_map/all_gather | solution.py:152
  51.3 3.2 %collective-permute-start.8 = (f32[3,16,16,1]{3,2,0,1:T(8,128)S(1)}, f32[3,16,16,1]{3,2,0,1:T(8,128)S(1)}, u32[]{:S(2)}, u32[]{:S(2)}) collective-permute-start(f32[3,16,16,1]{3,2,0,1:T(8,128)S(1)} %get-tuple-element.180), channel_id=1, source_target_pairs={{0,8},{8,16},{16,24},{1,9},{9,17},{17,25},{2,10},{10,18},{18,26},{... | collective-permute-start | bytes 9224 | tf_op jit(solution)/shard_map/ppermute | solution.py:9
  54.5 1.3 %collective-permute-start.9 = (f32[3,16,16,1]{3,2,0,1:T(8,128)S(1)}, f32[3,16,16,1]{3,2,0,1:T(8,128)S(1)}, u32[]{:S(2)}, u32[]{:S(2)}) collective-permute-start(f32[3,16,16,1]{3,2,0,1:T(8,128)S(1)} %get-tuple-element.179), channel_id=1, source_target_pairs={{8,0},{16,8},{24,16},{9,1},{17,9},{25,17},{10,2},{18,10},{26,18},{... | collective-permute-start | bytes 9224 | tf_op jit(solution)/shard_map/ppermute | solution.py:14
  55.8 10.3 %collective-permute-start.6 = (f32[3,16,1,128]{3,2,0,1:T(1,128)S(1)}, f32[3,16,1,128]{3,2,0,1:T(1,128)S(1)}, u32[]{:S(2)}, u32[]{:S(2)}) collective-permute-start(f32[3,16,1,128]{3,2,0,1:T(1,128)S(1)} %get-tuple-element.184), channel_id=1, source_target_pairs={{0,32},{32,64},{64,96},{96,128},{128,160},{160,192},{192,224},{1,3... | collective-permute-start | bytes 73736 | tf_op jit(solution)/shard_map/ppermute | solution.py:9
  66.1 1.9 %collective-permute-start.7 = (f32[3,16,1,128]{3,2,0,1:T(1,128)S(1)}, f32[3,16,1,128]{3,2,0,1:T(1,128)S(1)}, u32[]{:S(2)}, u32[]{:S(2)}) collective-permute-start(f32[3,16,1,128]{3,2,0,1:T(1,128)S(1)} %get-tuple-element.183), channel_id=1, source_target_pairs={{32,0},{64,32},{96,64},{128,96},{160,128},{192,160},{224,192},{33,... | collective-permute-start | bytes 73736 | tf_op jit(solution)/shard_map/ppermute | solution.py:14
  68.2 3.1 %collective-permute-done.7 = f32[3,16,1,128]{3,2,0,1:T(1,128)S(1)} collective-permute-done((f32[3,16,1,128]{3,2,0,1:T(1,128)S(1)}, f32[3,16,1,128]{3,2,0,1:T(1,128)S(1)}, u32[]{:S(2)}, u32[]{:S(2)}) %collective-permute-start.7) | collective-permute-done | bytes 24608 | tf_op jit(solution)/shard_map/ppermute | solution.py:14
  72.3 18.8 %all-gather.1 = f32[16,3,16,128]{3,2,1,0:T(8,128)S(1)} all-gather(f32[2,3,16,128]{3,2,1,0:T(8,128)S(1)} %pad_maximum_fusion.17), channel_id=3, replica_groups=mesh['gx'=8,'gy'=4,'gz'=8] {'gz'}, dimensions={0}, use_global_device_ids=true | all-gather | bytes 442368 | tf_op jit(solution)/shard_map/all_gather | solution.py:198
  92.0 4.1 %collective-permute-start.12 = (f32[3,16,16,1]{3,2,0,1:T(8,128)S(1)}, f32[3,16,16,1]{3,2,0,1:T(8,128)S(1)}, u32[]{:S(2)}, u32[]{:S(2)}) collective-permute-start(f32[3,16,16,1]{3,2,0,1:T(8,128)S(1)} %get-tuple-element.169), channel_id=1, source_target_pairs={{0,8},{8,16},{16,24},{1,9},{9,17},{17,25},{2,10},{10,18},{18,26},{... | collective-permute-start | bytes 9224 | tf_op jit(solution)/shard_map/ppermute | solution.py:9
  96.2 1.3 %collective-permute-start.13 = (f32[3,16,16,1]{3,2,0,1:T(8,128)S(1)}, f32[3,16,16,1]{3,2,0,1:T(8,128)S(1)}, u32[]{:S(2)}, u32[]{:S(2)}) collective-permute-start(f32[3,16,16,1]{3,2,0,1:T(8,128)S(1)} %get-tuple-element.168), channel_id=1, source_target_pairs={{8,0},{16,8},{24,16},{9,1},{17,9},{25,17},{10,2},{18,10},{26,18},{... | collective-permute-start | bytes 9224 | tf_op jit(solution)/shard_map/ppermute | solution.py:14
  97.5 8.9 %collective-permute-start.10 = (f32[3,16,1,128]{3,2,0,1:T(1,128)S(1)}, f32[3,16,1,128]{3,2,0,1:T(1,128)S(1)}, u32[]{:S(2)}, u32[]{:S(2)}) collective-permute-start(f32[3,16,1,128]{3,2,0,1:T(1,128)S(1)} %get-tuple-element.173), channel_id=1, source_target_pairs={{0,32},{32,64},{64,96},{96,128},{128,160},{160,192},{192,224},{1,3... | collective-permute-start | bytes 73736 | tf_op jit(solution)/shard_map/ppermute | solution.py:9
  106.4 1.9 %collective-permute-start.11 = (f32[3,16,1,128]{3,2,0,1:T(1,128)S(1)}, f32[3,16,1,128]{3,2,0,1:T(1,128)S(1)}, u32[]{:S(2)}, u32[]{:S(2)}) collective-permute-start(f32[3,16,1,128]{3,2,0,1:T(1,128)S(1)} %get-tuple-element.172), channel_id=1, source_target_pairs={{32,0},{64,32},{96,64},{128,96},{160,128},{192,160},{224,192},{33,... | collective-permute-start | bytes 73736 | tf_op jit(solution)/shard_map/ppermute | solution.py:14
  108.4 0.8 copy.204
  109.2 2.4 %collective-permute-done.11 = f32[3,16,1,128]{3,2,0,1:T(1,128)S(1)} collective-permute-done((f32[3,16,1,128]{3,2,0,1:T(1,128)S(1)}, f32[3,16,1,128]{3,2,0,1:T(1,128)S(1)}, u32[]{:S(2)}, u32[]{:S(2)}) %collective-permute-start.11) | collective-permute-done | bytes 24608 | tf_op jit(solution)/shard_map/ppermute | solution.py:14
  111.5 0.5 fusion.11
  112.0 0.8 copy.205
  (142 shorter events, 7.0 us)
Async XLA Ops:
  0.6 1.3 %copy-start = (f32[3,16]{1,0:T(4,128)S(1)}, f32[3,16]{1,0:T(4,128)}, u32[]{:S(2)}) copy-start(f32[3,16]{1,0:T(4,128)} %param.4) | copy-start | bytes 580
  2.9 15.4 %collective-permute-start.2 = (f32[16,16,1]{2,1,0:T(8,128)S(1)}, f32[16,16,1]{2,1,0:T(8,128)S(1)}, u32[]{:S(2)}, u32[]{:S(2)}) collective-permute-start(f32[16,16,1]{2,1,0:T(8,128)S(1)} %get-tuple-element.220), channel_id=1, source_target_pairs={{8,0},{16,8},{24,16},{9,1},{17,9},{25,17},{10,2},{18,10},{26,18},{... | collective-permute-start | bytes 3080 | tf_op jit(solution)/shard_map/ppermute | solution.py:14
  4.2 18.1 %collective-permute-start.3 = (f32[16,16,1]{2,1,0:T(8,128)S(1)}, f32[16,16,1]{2,1,0:T(8,128)S(1)}, u32[]{:S(2)}, u32[]{:S(2)}) collective-permute-start(f32[16,16,1]{2,1,0:T(8,128)S(1)} %get-tuple-element.219), channel_id=1, source_target_pairs={{0,8},{8,16},{16,24},{1,9},{9,17},{17,25},{2,10},{10,18},{18,26},{... | collective-permute-start | bytes 3080 | tf_op jit(solution)/shard_map/ppermute | solution.py:9
  8.9 13.4 %collective-permute-start = (f32[16,1,128]{2,1,0:T(1,128)S(1)}, f32[16,1,128]{2,1,0:T(1,128)S(1)}, u32[]{:S(2)}, u32[]{:S(2)}) collective-permute-start(f32[16,1,128]{2,1,0:T(1,128)S(1)} %get-tuple-element.218), channel_id=1, source_target_pairs={{32,0},{64,32},{96,64},{128,96},{160,128},{192,160},{224,192},{33,... | collective-permute-start | bytes 24584 | tf_op jit(solution)/shard_map/ppermute | solution.py:14
  14.0 8.4 %collective-permute-start.1 = (f32[16,1,128]{2,1,0:T(1,128)S(1)}, f32[16,1,128]{2,1,0:T(1,128)S(1)}, u32[]{:S(2)}, u32[]{:S(2)}) collective-permute-start(f32[16,1,128]{2,1,0:T(1,128)S(1)} %get-tuple-element.217), channel_id=1, source_target_pairs={{0,32},{32,64},{64,96},{96,128},{128,160},{160,192},{192,224},{1,3... | collective-permute-start | bytes 24584 | tf_op jit(solution)/shard_map/ppermute | solution.py:9
  15.9 6.4 %collective-permute-start.4 = (f32[1,16,128]{2,1,0:T(8,128)S(1)}, f32[1,16,128]{2,1,0:T(8,128)S(1)}, u32[]{:S(2)}, u32[]{:S(2)}) collective-permute-start(f32[1,16,128]{2,1,0:T(8,128)S(1)} %get-tuple-element.192), channel_id=1, source_target_pairs={{1,0},{2,1},{3,2},{4,3},{5,4},{6,5},{7,6},{9,8},{10,9},{11,10},{12... | collective-permute-start | bytes 24584 | tf_op jit(solution)/shard_map/ppermute | solution.py:14
  17.4 0.7 copy-start.1
  18.3 4.8 %collective-permute-start.5 = (f32[1,16,128]{2,1,0:T(8,128)S(1)}, f32[1,16,128]{2,1,0:T(8,128)S(1)}, u32[]{:S(2)}, u32[]{:S(2)}) collective-permute-start(f32[1,16,128]{2,1,0:T(8,128)S(1)} %get-tuple-element.191), channel_id=1, source_target_pairs={{0,1},{1,2},{2,3},{3,4},{4,5},{5,6},{6,7},{8,9},{9,10},{10,11},{11... | collective-permute-start | bytes 24584 | tf_op jit(solution)/shard_map/ppermute | solution.py:9
  51.3 16.9 %collective-permute-start.8 = (f32[3,16,16,1]{3,2,0,1:T(8,128)S(1)}, f32[3,16,16,1]{3,2,0,1:T(8,128)S(1)}, u32[]{:S(2)}, u32[]{:S(2)}) collective-permute-start(f32[3,16,16,1]{3,2,0,1:T(8,128)S(1)} %get-tuple-element.180), channel_id=1, source_target_pairs={{0,8},{8,16},{16,24},{1,9},{9,17},{17,25},{2,10},{10,18},{18,26},{... | collective-permute-start | bytes 9224 | tf_op jit(solution)/shard_map/ppermute | solution.py:9
  54.5 13.7 %collective-permute-start.9 = (f32[3,16,16,1]{3,2,0,1:T(8,128)S(1)}, f32[3,16,16,1]{3,2,0,1:T(8,128)S(1)}, u32[]{:S(2)}, u32[]{:S(2)}) collective-permute-start(f32[3,16,16,1]{3,2,0,1:T(8,128)S(1)} %get-tuple-element.179), channel_id=1, source_target_pairs={{8,0},{16,8},{24,16},{9,1},{17,9},{25,17},{10,2},{18,10},{26,18},{... | collective-permute-start | bytes 9224 | tf_op jit(solution)/shard_map/ppermute | solution.py:14
  55.8 12.4 %collective-permute-start.6 = (f32[3,16,1,128]{3,2,0,1:T(1,128)S(1)}, f32[3,16,1,128]{3,2,0,1:T(1,128)S(1)}, u32[]{:S(2)}, u32[]{:S(2)}) collective-permute-start(f32[3,16,1,128]{3,2,0,1:T(1,128)S(1)} %get-tuple-element.184), channel_id=1, source_target_pairs={{0,32},{32,64},{64,96},{96,128},{128,160},{160,192},{192,224},{1,3... | collective-permute-start | bytes 73736 | tf_op jit(solution)/shard_map/ppermute | solution.py:9
  66.1 5.1 %collective-permute-start.7 = (f32[3,16,1,128]{3,2,0,1:T(1,128)S(1)}, f32[3,16,1,128]{3,2,0,1:T(1,128)S(1)}, u32[]{:S(2)}, u32[]{:S(2)}) collective-permute-start(f32[3,16,1,128]{3,2,0,1:T(1,128)S(1)} %get-tuple-element.183), channel_id=1, source_target_pairs={{32,0},{64,32},{96,64},{128,96},{160,128},{192,160},{224,192},{33,... | collective-permute-start | bytes 73736 | tf_op jit(solution)/shard_map/ppermute | solution.py:14
  92.0 17.1 %collective-permute-start.12 = (f32[3,16,16,1]{3,2,0,1:T(8,128)S(1)}, f32[3,16,16,1]{3,2,0,1:T(8,128)S(1)}, u32[]{:S(2)}, u32[]{:S(2)}) collective-permute-start(f32[3,16,16,1]{3,2,0,1:T(8,128)S(1)} %get-tuple-element.169), channel_id=1, source_target_pairs={{0,8},{8,16},{16,24},{1,9},{9,17},{17,25},{2,10},{10,18},{18,26},{... | collective-permute-start | bytes 9224 | tf_op jit(solution)/shard_map/ppermute | solution.py:9
  96.2 13.0 %collective-permute-start.13 = (f32[3,16,16,1]{3,2,0,1:T(8,128)S(1)}, f32[3,16,16,1]{3,2,0,1:T(8,128)S(1)}, u32[]{:S(2)}, u32[]{:S(2)}) collective-permute-start(f32[3,16,16,1]{3,2,0,1:T(8,128)S(1)} %get-tuple-element.168), channel_id=1, source_target_pairs={{8,0},{16,8},{24,16},{9,1},{17,9},{25,17},{10,2},{18,10},{26,18},{... | collective-permute-start | bytes 9224 | tf_op jit(solution)/shard_map/ppermute | solution.py:14
  97.5 11.7 %collective-permute-start.10 = (f32[3,16,1,128]{3,2,0,1:T(1,128)S(1)}, f32[3,16,1,128]{3,2,0,1:T(1,128)S(1)}, u32[]{:S(2)}, u32[]{:S(2)}) collective-permute-start(f32[3,16,1,128]{3,2,0,1:T(1,128)S(1)} %get-tuple-element.173), channel_id=1, source_target_pairs={{0,32},{32,64},{64,96},{96,128},{128,160},{160,192},{192,224},{1,3... | collective-permute-start | bytes 73736 | tf_op jit(solution)/shard_map/ppermute | solution.py:9
  106.4 5.1 %collective-permute-start.11 = (f32[3,16,1,128]{3,2,0,1:T(1,128)S(1)}, f32[3,16,1,128]{3,2,0,1:T(1,128)S(1)}, u32[]{:S(2)}, u32[]{:S(2)}) collective-permute-start(f32[3,16,1,128]{3,2,0,1:T(1,128)S(1)} %get-tuple-element.172), channel_id=1, source_target_pairs={{32,0},{64,32},{96,64},{128,96},{160,128},{192,160},{224,192},{33,... | collective-permute-start | bytes 73736 | tf_op jit(solution)/shard_map/ppermute | solution.py:14
